TPU v7x, 32 devices: a whole 2x2x4 slice. The times are simulated.
32 devices in a mesh: tm: 4 (over z), tile: 2 (over y), clip: 4 (over x, core).
Axes of the slice: x: 2, y: 2, z: 4, core: 2. Of those that a mesh axis runs over, the one named last changes fastest.
Arguments:
- latents: bfloat16 [32, 16, 128, 256], P(('clip', 'tm'), 'tile'), parts along dimension 0, may hold values from -40 to 40
- norm1_gain: float32 [256], replicated, may hold values from 0.1 to 1.9
- conv1_weight: bfloat16 [27, 256, 256], P(None, None, ('tm', 'tile')), may hold values from -0.078125 to 0.078125
- conv1_bias: float32 [256], replicated, may hold values from -3 to 3
- norm2_gain: float32 [256], replicated, may hold values from 0.1 to 1.9
- conv2_weight: bfloat16 [27, 256, 256], P(None, None, ('tm', 'tile')), may hold values from -0.078125 to 0.078125
- conv2_bias: float32 [256], replicated, may hold values from -3 to 3
Outputs:
- decoded: bfloat16 [32, 16, 128, 256], P(('clip', 'tm'), 'tile'), parts along dimension 0
There are 4 independent parts, one for each index of `clip`. A program takes and returns all parts, laid end to end along the dimension named above; an argument that names none is the same for every part. Nothing has to cross between parts.
All inputs are finite; a program needn't handle non-finite values.
Results may differ from a plain program's by a relative error of at most 0.003.
Values may be sent and summed in bfloat16 or wider, within the bound.
No kernel may reach another device: no remote copies, remote signals or barrier semaphores. Data moves between devices by JAX's collectives and lax.ppermute only.
A program may use at most 64 MiB of HBM per device.

v0:
```python
import jax
import jax.numpy as jnp
from jax import lax
from jax.sharding import PartitionSpec as P

GROUPS = 32
epsilon = 1e-06


def from_behind(value, axis, steps):
    count = lax.axis_size(axis)
    first, last = (max(0, -steps), min(count, count - steps))
    return lax.ppermute(value, axis, [(source, source + steps) for source in range(first, last)])


def padded_2(block, sides, width):
    for axis, dim in sides:
        count = lax.axis_size(axis)
        forward = [(i, i + 1) for i in range(count - 1)]
        backward = [(target, source) for source, target in forward]
        low = lax.ppermute(
            lax.slice_in_dim(block, block.shape[dim] - width, None, axis=dim), axis, forward
        )
        high = lax.ppermute(lax.slice_in_dim(block, 0, width, axis=dim), axis, backward)
        block = jnp.concatenate([low, block, high], axis=dim)
    return block


def normalize(inputs_f, gain_vec):
    frames, rows_here, columns, channels = inputs_f.shape
    grouped = inputs_f.reshape(frames, rows_here * columns, GROUPS, channels // GROUPS)
    counted = float(rows_here * columns * (channels // GROUPS) * lax.axis_size("tile"))
    totals = lax.psum(jnp.sum(grouped, axis=(1, 3)), "tile")
    group_mean = totals / counted
    centered = grouped - group_mean[:, None, :, None]
    spread = lax.psum(jnp.sum(centered * centered, axis=(1, 3)), "tile")
    group_var = spread / counted
    normed = (centered * lax.rsqrt(group_var + epsilon)[:, None, :, None]).reshape(
        inputs_f.shape
    ) * gain_vec
    return jax.nn.silu(normed).astype(jnp.bfloat16)


def widen_cols(block, columns):
    padded = jnp.pad(block, ((0, 0), (0, 0), (1, 1), (0, 0)))
    return jnp.concatenate(
        [padded[:, :, shift_col : shift_col + columns] for shift_col in range(3)], axis=-1
    )


def convolve(activated, weight_shard, bias_vec):
    frames, rows_here, columns, channels = activated.shape
    cached = from_behind(activated, "tm", 1)
    extended = jnp.concatenate([cached, activated], axis=0)
    rimmed = padded_2(extended, (("tile", 1),), 1)
    shard_piece = lax.all_gather(weight_shard, ("tm", "tile"), axis=2, tiled=True)
    outputs_here = shard_piece.shape[2]
    kernel = shard_piece.reshape(3, 3, 3 * channels, outputs_here)
    summed = jnp.zeros((frames, rows_here, columns, outputs_here), jnp.float32)
    widened = widen_cols(rimmed, columns)
    for frame_off in range(3):
        for row_off in range(3):
            summed = summed + jnp.einsum(
                "trwk,kn->trwn",
                widened[frame_off : frame_off + frames, row_off : row_off + rows_here],
                kernel[frame_off, row_off],
                preferred_element_type=jnp.float32,
            )
    return summed + bias_vec


def shards(latents, norm1_gain, conv1_weight, conv1_bias, norm2_gain, conv2_weight, conv2_bias):
    inputs_f = latents.astype(jnp.float32)
    hidden = convolve(normalize(inputs_f, norm1_gain), conv1_weight, conv1_bias).astype(
        jnp.bfloat16
    )
    second = convolve(normalize(hidden.astype(jnp.float32), norm2_gain), conv2_weight, conv2_bias)
    return (inputs_f + second).astype(jnp.bfloat16)


def solution(mesh):
    placed = (
        P(("clip", "tm"), "tile", None, None),
        P(),
        P(None, None, ("tm", "tile")),
        P(),
        P(),
        P(None, None, ("tm", "tile")),
        P(),
    )
    return jax.shard_map(
        shards,
        mesh=mesh,
        in_specs=placed,
        out_specs=P(("clip", "tm"), "tile", None, None),
        check_vma=False,
    )
```

profile of v0, /device:TPU:24, one launch (start us, length us, event | category | flops | bytes accessed | tf_op | source)
XLA Modules:
  0.0 209.7 jit_solution(16347411806970437076)
XLA Ops:
  7.3 1.4 convert_reduce_fusion
  8.9 4.9 %psum.28 = f32[2,32]{1,0:T(2,128)S(1)} all-reduce(f32[2,32]{1,0:T(2,128)S(1)} %reduce_sum.51), channel_id=1, replica_groups=mesh['tm'=4,'tile'=2,'clip'=4] {'tile'}, use_global_device_ids=true, to_apply=%region_2.0 | all-reduce | flops 64 | bytes 512 | tf_op jit(solution)/shard_map/psum | solution.py:33
  14.0 1.5 fusion.15
  15.7 4.9 %psum.29 = f32[2,32]{1,0:T(2,128)S(1)} all-reduce(f32[2,32]{1,0:T(2,128)S(1)} %reduce_sum.54), channel_id=1, replica_groups=mesh['tm'=4,'tile'=2,'clip'=4] {'tile'}, use_global_device_ids=true, to_apply=%region_5.6 | all-reduce | flops 64 | bytes 512 | tf_op jit(solution)/shard_map/psum | solution.py:36
  20.8 1.3 fusion.22
  22.2 1.3 collective-permute-start
  23.5 48.3 %collective-permute-done = bf16[2,8,128,256]{3,2,1,0:T(8,128)(2,1)S(1)} collective-permute-done((bf16[2,8,128,256]{3,2,1,0:T(8,128)(2,1)S(1)}, bf16[2,8,128,256]{3,2,1,0:T(8,128)(2,1)S(1)}, u32[]{:S(2)}, u32[]{:S(2)}) %collective-permute-start) | collective-permute-done | bytes 1048608 | tf_op jit(solution)/shard_map/ppermute | solution.py:13
  72.6 3.4 %collective-permute-start.1 = (bf16[4,1,128,256]{3,2,1,0:T(8,128)(2,1)}, bf16[4,1,128,256]{3,2,1,0:T(8,128)(2,1)S(1)}, u32[]{:S(2)}, u32[]{:S(2)}) collective-permute-start(bf16[4,1,128,256]{3,2,1,0:T(8,128)(2,1)} %get-tuple-element.11), channel_id=1, source_target_pairs={{0,4},{1,5},{2,6},{3,7},{8,12},{9,13},{10,14},{11,15},{16,20},{17,... | collective-permute-start | bytes 786440 | tf_op jit(solution)/shard_map/ppermute | solution.py:21
  76.0 1.3 collective-permute-start.2
  77.3 2.8 %collective-permute-done.1 = bf16[4,1,128,256]{3,2,1,0:T(8,128)(2,1)S(1)} collective-permute-done((bf16[4,1,128,256]{3,2,1,0:T(8,128)(2,1)}, bf16[4,1,128,256]{3,2,1,0:T(8,128)(2,1)S(1)}, u32[]{:S(2)}, u32[]{:S(2)}) %collective-permute-start.1) | collective-permute-done | bytes 262176 | tf_op jit(solution)/shard_map/ppermute | solution.py:21
  80.2 4.4 %collective-permute-done.2 = bf16[4,1,128,256]{3,2,1,0:T(8,128)(2,1)} collective-permute-done((bf16[4,1,128,256]{3,2,1,0:T(8,128)(2,1)}, bf16[4,1,128,256]{3,2,1,0:T(8,128)(2,1)}, u32[]{:S(2)}, u32[]{:S(2)}) %collective-permute-start.2) | collective-permute-done | bytes 262176 | tf_op jit(solution)/shard_map/ppermute | solution.py:24
  84.6 2.1 %fusion.8 = bf16[4,10,130,256]{3,2,1,0:T(8,128)(2,1)S(1)} fusion(bf16[4,1,128,256]{3,2,1,0:T(8,128)(2,1)} %collective-permute-done.2, bf16[4,1,128,256]{3,2,1,0:T(8,128)(2,1)S(1)} %collective-permute-done.1, bf16[2,8,128,256]{3,2,1,0:T(8,128)(2,1)S(1)} %fusion.22, bf16[2,8,128,256]{3,2,1,0:T(8,128)(2,1)S(1)} %collective-permute-done), kind=kLoop, calls=%fused_computation.17 | loop fusion | flops 19968000 | bytes 5283840 | tf_op jit(solution)/shard_map/concatenate | solution.py:25
  86.7 1.9 fusion.49
  88.6 4.7 %pad_maximum_fusion = bf16[4,10,128,768]{3,2,1,0:T(8,128)(2,1)} fusion(bf16[4,10,128,256]{3,2,1,0:T(8,128)(2,1)S(1)} %get-tuple-element.8, bf16[4,1,128,256]{3,2,1,0:T(8,128)(2,1)} %collective-permute-done.2, bf16[2,8,128,256]{3,2,1,0:T(8,128)(2,1)S(1)} %fusion.22, bf16[2,8,128,256]{3,2,1,0:T(8,128)(2,1)S(1)} %collective-permute-done, ...), kind=kLoop, calls=%fused_computation.2 | loop fusion | flops 47185920 | bytes 15728640 | tf_op jit(solution)/shard_map/concatenate | solution.py:46
  93.3 5.8 %copy.10 = bf16[27,256,256]{2,1,0:T(8,128)(2,1)} copy(bf16[27,256,256]{1,2,0:T(8,128)(2,1)} %all-gather.3.cloned.1.call-done) | data formatting | bytes 7077888 | tf_op jit(solution)/shard_map/all_gather | solution.py:56
  99.0 3.1 %fusion.40 = f32[2,8,128,256]{3,2,1,0:T(8,128)S(1)} fusion(bf16[4,10,128,768]{3,2,1,0:T(8,128)(2,1)} %pad_maximum_fusion, bf16[3,3,768,256]{3,2,1,0:T(8,128)(2,1)} %bitcast.157), kind=kOutput, calls=%fused_computation.63 | convolution fusion | flops 805306368 | bytes 10354688 | tf_op jit(solution)/shard_map/trwk,kn->trwn/dot_general | solution.py:63
  102.2 3.7 %fusion.41 = f32[2,8,128,256]{3,2,1,0:T(8,128)S(1)} fusion(bf16[4,10,128,768]{3,2,1,0:T(8,128)(2,1)} %pad_maximum_fusion, bf16[3,3,768,256]{3,2,1,0:T(8,128)(2,1)S(1)} %bitcast.158), kind=kOutput, calls=%fused_computation.65 | convolution fusion | flops 805306368 | bytes 10354688 | tf_op jit(solution)/shard_map/trwk,kn->trwn/dot_general | solution.py:63
  111.9 1.5 convert_reduce_fusion.1
  113.6 5.1 %psum.30 = f32[2,32]{1,0:T(2,128)S(1)} all-reduce(f32[2,32]{1,0:T(2,128)S(1)} %reduce_sum.72), channel_id=1, replica_groups=mesh['tm'=4,'tile'=2,'clip'=4] {'tile'}, use_global_device_ids=true, to_apply=%region_8.9 | all-reduce | flops 64 | bytes 512 | tf_op jit(solution)/shard_map/psum | solution.py:33
  119.3 4.9 %psum.31 = f32[2,32]{1,0:T(2,128)S(1)} all-reduce(f32[2,32]{1,0:T(2,128)S(1)} %reduce_sum.75), channel_id=1, replica_groups=mesh['tm'=4,'tile'=2,'clip'=4] {'tile'}, use_global_device_ids=true, to_apply=%region_11.12 | all-reduce | flops 64 | bytes 512 | tf_op jit(solution)/shard_map/psum | solution.py:36
  125.1 1.3 collective-permute-start.3
  126.4 46.1 %collective-permute-done.3 = bf16[2,8,128,256]{3,2,1,0:T(8,128)(2,1)S(1)} collective-permute-done((bf16[2,8,128,256]{3,2,1,0:T(8,128)(2,1)S(1)}, bf16[2,8,128,256]{3,2,1,0:T(8,128)(2,1)S(1)}, u32[]{:S(2)}, u32[]{:S(2)}) %collective-permute-start.3) | collective-permute-done | bytes 1048608 | tf_op jit(solution)/shard_map/ppermute | solution.py:13
  173.4 3.4 %collective-permute-start.4 = (bf16[4,1,128,256]{3,2,1,0:T(8,128)(2,1)}, bf16[4,1,128,256]{3,2,1,0:T(8,128)(2,1)S(1)}, u32[]{:S(2)}, u32[]{:S(2)}) collective-permute-start(bf16[4,1,128,256]{3,2,1,0:T(8,128)(2,1)} %get-tuple-element.9), channel_id=1, source_target_pairs={{0,4},{1,5},{2,6},{3,7},{8,12},{9,13},{10,14},{11,15},{16,20},{17,... | collective-permute-start | bytes 786440 | tf_op jit(solution)/shard_map/ppermute | solution.py:21
  176.7 1.3 collective-permute-start.5
  178.1 5.7 %copy.11 = bf16[27,256,256]{2,1,0:T(8,128)(2,1)} copy(bf16[27,256,256]{1,2,0:T(8,128)(2,1)} %all-gather.5.cloned.1.call-done) | data formatting | bytes 7077888 | tf_op jit(solution)/shard_map/all_gather | solution.py:56
  183.8 2.0 collective-permute-done.5
  185.8 2.1 %select_maximum_fusion = bf16[4,10,130,256]{3,2,1,0:T(8,128)(2,1)S(1)} fusion(bf16[4,1,128,256]{3,2,1,0:T(8,128)(2,1)} %collective-permute-done.5, bf16[4,1,128,256]{3,2,1,0:T(8,128)(2,1)S(1)} %collective-permute-done.4, bf16[2,8,128,256]{3,2,1,0:T(8,128)(2,1)S(1)} %fusion.30, bf16[2,8,128,256]{3,2,1,0:T(8,128)(2,1)S(1)} %collective-permute-done.3), kind=kLoop, calls=%fused_computation.8 | loop fusion | flops 19968000 | bytes 5283840 | tf_op jit(solution)/shard_map/concatenate | solution.py:25
  187.9 1.9 fusion.48
  189.8 2.4 %pad_maximum_fusion.1 = bf16[4,10,128,768]{3,2,1,0:T(8,128)(2,1)S(1)} fusion(bf16[4,10,128,256]{3,2,1,0:T(8,128)(2,1)S(1)} %get-tuple-element.6, bf16[4,1,128,256]{3,2,1,0:T(8,128)(2,1)} %collective-permute-done.5, bf16[2,8,128,256]{3,2,1,0:T(8,128)(2,1)S(1)} %fusion.30, bf16[2,8,128,256]{3,2,1,0:T(8,128)(2,1)S(1)} %collective-permute-done.3, ...), kind=kLoop, calls=%fused_computation.3 | loop fusion | flops 47185920 | bytes 15728640 | tf_op jit(solution)/shard_map/concatenate | solution.py:46
  197.2 1.0 fusion.37
  198.2 1.0 fusion.38
  200.2 2.6 %fusion.31 = bf16[2,8,128,256]{3,2,1,0:T(8,128)(2,1)} fusion(bf16[2,8,128,256]{3,2,1,0:T(8,128)(2,1)S(1)} %copy-done.1, f32[2,8,128,256]{3,2,1,0:T(8,128)S(1)} %fusion.32, f32[2,8,128,256]{3,2,1,0:T(8,128)S(1)} %fusion.33, f32[2,8,128,256]{3,2,1,0:T(8,128)S(1)} %fusion.34, f32[2,8,128,256]{3,2,1,0:T(8,128)S(1)} %fusion.35, ...), kind=kOutput, calls=%fused_computation.42 | convolution fusion | flops 811597824 | bytes 27132928 | tf_op jit(solution)/shard_map/trwk,kn->trwn/dot_general | solution.py:63
  (57 shorter events, 16.6 us)
Async XLA Ops:
  6.5 14.3 %copy-start.1 = (bf16[2,8,128,256]{3,2,1,0:T(8,128)(2,1)S(1)}, bf16[2,8,128,256]{3,2,1,0:T(8,128)(2,1)}, u32[]{:S(2)}) copy-start(bf16[2,8,128,256]{3,2,1,0:T(8,128)(2,1)} %param.7) | copy-start | bytes 3145732
  6.5 86.7 %all-gather.3.cloned.1.call-start = ((), (), s32[]{:S(2)}) async-start(), calls=%async_computation | async-start | bytes 3981312 | tf_op jit(solution)/shard_map/all_gather | solution.py:56
  7.3 170.8 %all-gather.5.cloned.1.call-start = ((), (), s32[]{:S(2)}) async-start(), calls=%async_computation.1 | async-start | bytes 3981312 | tf_op jit(solution)/shard_map/all_gather | solution.py:56
  22.2 49.6 %collective-permute-start = (bf16[2,8,128,256]{3,2,1,0:T(8,128)(2,1)S(1)}, bf16[2,8,128,256]{3,2,1,0:T(8,128)(2,1)S(1)}, u32[]{:S(2)}, u32[]{:S(2)}) collective-permute-start(bf16[2,8,128,256]{3,2,1,0:T(8,128)(2,1)S(1)} %fusion.22), channel_id=1, source_target_pairs={{0,8},{8,16},{16,24},{1,9},{9,17},{17,25},{2,10},{10,18},{18,26},{... | collective-permute-start | bytes 3145736 | tf_op jit(solution)/shard_map/ppermute | solution.py:13
  72.6 7.6 %collective-permute-start.1 = (bf16[4,1,128,256]{3,2,1,0:T(8,128)(2,1)}, bf16[4,1,128,256]{3,2,1,0:T(8,128)(2,1)S(1)}, u32[]{:S(2)}, u32[]{:S(2)}) collective-permute-start(bf16[4,1,128,256]{3,2,1,0:T(8,128)(2,1)} %get-tuple-element.11), channel_id=1, source_target_pairs={{0,4},{1,5},{2,6},{3,7},{8,12},{9,13},{10,14},{11,15},{16,20},{17,... | collective-permute-start | bytes 786440 | tf_op jit(solution)/shard_map/ppermute | solution.py:21
  76.0 8.6 %collective-permute-start.2 = (bf16[4,1,128,256]{3,2,1,0:T(8,128)(2,1)}, bf16[4,1,128,256]{3,2,1,0:T(8,128)(2,1)}, u32[]{:S(2)}, u32[]{:S(2)}) collective-permute-start(bf16[4,1,128,256]{3,2,1,0:T(8,128)(2,1)} %get-tuple-element.12), channel_id=1, source_target_pairs={{4,0},{5,1},{6,2},{7,3},{12,8},{13,9},{14,10},{15,11},{20,16},{21,... | collective-permute-start | bytes 786440 | tf_op jit(solution)/shard_map/ppermute | solution.py:24
  99.0 3.1 %copy-start.3 = (bf16[27,256,256]{2,1,0:T(8,128)(2,1)S(1)}, bf16[27,256,256]{2,1,0:T(8,128)(2,1)}, u32[]{:S(2)}) copy-start(bf16[27,256,256]{2,1,0:T(8,128)(2,1)} %copy.10) | copy-start | bytes 10616836
  99.0 6.8 %copy-start = (bf16[4,10,128,768]{3,2,1,0:T(8,128)(2,1)S(1)}, bf16[4,10,128,768]{3,2,1,0:T(8,128)(2,1)}, u32[]{:S(2)}) copy-start(bf16[4,10,128,768]{3,2,1,0:T(8,128)(2,1)} %pad_maximum_fusion) | copy-start | bytes 23592964
  110.8 1.0 copy-start.4
  111.8 12.6 %copy-start.6 = (f32[256]{0:T(256)S(1)}, f32[256]{0:T(256)}, u32[]{:S(2)}) copy-start(f32[256]{0:T(256)} %param.11) | copy-start | bytes 3076
  125.1 47.4 %collective-permute-start.3 = (bf16[2,8,128,256]{3,2,1,0:T(8,128)(2,1)S(1)}, bf16[2,8,128,256]{3,2,1,0:T(8,128)(2,1)S(1)}, u32[]{:S(2)}, u32[]{:S(2)}) collective-permute-start(bf16[2,8,128,256]{3,2,1,0:T(8,128)(2,1)S(1)} %fusion.30), channel_id=1, source_target_pairs={{0,8},{8,16},{16,24},{1,9},{9,17},{17,25},{2,10},{10,18},{18,26},{... | collective-permute-start | bytes 3145736 | tf_op jit(solution)/shard_map/ppermute | solution.py:13
  173.4 10.5 %collective-permute-start.4 = (bf16[4,1,128,256]{3,2,1,0:T(8,128)(2,1)}, bf16[4,1,128,256]{3,2,1,0:T(8,128)(2,1)S(1)}, u32[]{:S(2)}, u32[]{:S(2)}) collective-permute-start(bf16[4,1,128,256]{3,2,1,0:T(8,128)(2,1)} %get-tuple-element.9), channel_id=1, source_target_pairs={{0,4},{1,5},{2,6},{3,7},{8,12},{9,13},{10,14},{11,15},{16,20},{17,... | collective-permute-start | bytes 786440 | tf_op jit(solution)/shard_map/ppermute | solution.py:21
  176.7 9.1 %collective-permute-start.5 = (bf16[4,1,128,256]{3,2,1,0:T(8,128)(2,1)}, bf16[4,1,128,256]{3,2,1,0:T(8,128)(2,1)}, u32[]{:S(2)}, u32[]{:S(2)}) collective-permute-start(bf16[4,1,128,256]{3,2,1,0:T(8,128)(2,1)} %get-tuple-element.10), channel_id=1, source_target_pairs={{4,0},{5,1},{6,2},{7,3},{12,8},{13,9},{14,10},{15,11},{20,16},{21,... | collective-permute-start | bytes 786440 | tf_op jit(solution)/shard_map/ppermute | solution.py:24
  189.8 2.4 %copy-start.2 = (bf16[27,256,256]{2,1,0:T(8,128)(2,1)S(1)}, bf16[27,256,256]{2,1,0:T(8,128)(2,1)}, u32[]{:S(2)}) copy-start(bf16[27,256,256]{2,1,0:T(8,128)(2,1)} %copy.11) | copy-start | bytes 10616836
  199.2 1.0 copy-start.5
Sparse Core Ops, SparseCore 0:
  9.5 76.6 all-gather.2
  88.4 73.8 all-gather.4
where the time goes:
time: 210 us
  waiting for transfers between devices  104 us (50%)
  matrix products  24.7 us (12%)
  blocking collectives  19.9 us (9%)
  other arithmetic  18.6 us (9%)
  local copies, waits for them, and re-layouts  16.3 us (8%)
  between operations  13.8 us (7%)
  starting transfers between devices  12 us (6%)
    ppermute x2, waiting for transfers between devices, from_behind(): lax.ppermute(value, axis, [(source, source + steps) for source in range(f...  94.4 us
    dot_general x18, matrix products, convolve(): jnp.einsum('trwk,kn->trwn', widened[frame_off:frame_off + frames, row_off...  24.7 us
    all_gather x2, local copies, waits for them, and re-layouts, convolve(): lax.all_gather(weight_shard, ('tm', 'tile'), axis=2, tiled=True)  11.5 us
    psum x2, blocking collectives, normalize(): totals = lax.psum(jnp.sum(grouped, axis=(1, 3)), 'tile')  10 us
    psum x2, blocking collectives, normalize(): spread = lax.psum(jnp.sum(centered * centered, axis=(1, 3)), 'tile')  9.86 us
    concatenate x2, other arithmetic, widen_cols(): jnp.concatenate([padded[:, :, shift_col:shift_col + columns] for shift_co...  7.11 us
    ppermute x2, starting transfers between devices, padded_2(): lax.ppermute(lax.slice_in_dim(block, block.shape[dim] - width, None, axis...  6.77 us
    ppermute x2, waiting for transfers between devices, padded_2(): lax.ppermute(lax.slice_in_dim(block, 0, width, axis=dim), axis, backward)  6.4 us
  transfers between devices with their start and end apart: 8, of which 5 were waited for; matrix products, arithmetic and copies ran while one was open for 20% of the time, Pallas kernels for 0%

commit v1 on v0

--- a/solution.py
+++ b/solution.py
@@ -53,7 +53,22 @@
     cached = from_behind(activated, "tm", 1)
     extended = jnp.concatenate([cached, activated], axis=0)
     rimmed = padded_2(extended, (("tile", 1),), 1)
-    shard_piece = lax.all_gather(weight_shard, ("tm", "tile"), axis=2, tiled=True)
+    ways, here, lap = (
+        lax.axis_size(("tm", "tile")),
+        lax.axis_index(("tm", "tile")),
+        weight_shard.shape[2],
+    )
+    line, have = (weight_shard, 1)
+    while have < ways:
+        line = jnp.concatenate(
+            [
+                line,
+                lax.ppermute(line, ("tm", "tile"), [(d, (d - have) % ways) for d in range(ways)]),
+            ],
+            axis=2,
+        )
+        have = 2 * have
+    shard_piece = jnp.roll(line, here * lap, axis=2)
     outputs_here = shard_piece.shape[2]
     kernel = shard_piece.reshape(3, 3, 3 * channels, outputs_here)
     summed = jnp.zeros((frames, rows_here, columns, outputs_here), jnp.float32)

time: 210 us -> 347 us (1.65)
  waiting for transfers between devices: 104 us -> 232 us
  other arithmetic: 18.6 us -> 34.2 us
  between operations: 13.8 us -> 0.45 us
    ppermute x0 -> x6, waiting for transfers between devices: none -> 148 us  [convolve(): lax.ppermute(line, ('tm', 'tile'), [(d, (d - have) % ways) for d in range...]
    ppermute x2, waiting for transfers between devices: 94.4 us -> 77.2 us  [from_behind(): lax.ppermute(value, axis, [(source, source + steps) for source in range(f...]
    concatenate x0 -> x5, other arithmetic: none -> 15.6 us  [the longest x1 11.1 us: convolve(): shard_piece = jnp.roll(line, here * lap, axis=2)]
    all_gather x2 -> x0, local copies, waits for them, and re-layouts: 11.5 us -> none  [convolve(): lax.all_gather(weight_shard, ('tm', 'tile'), axis=2, tiled=True)]
    dynamic_slice x0 -> x2, local copies, waits for them, and re-layouts: none -> 10.6 us  [convolve(): shard_piece = jnp.roll(line, here * lap, axis=2)]
    ppermute x0 -> x6, starting transfers between devices: none -> 5.81 us  [convolve(): lax.ppermute(line, ('tm', 'tile'), [(d, (d - have) % ways) for d in range...]
  transfers between devices with their start and end apart: 8 -> 12, of which waited for: 5 -> 9; matrix products, arithmetic and copies ran while one was open for 20% -> 6% of each run, Pallas kernels for 0% -> 0%
where the time goes in v1:
time: 347 us; the launch traced here: 346 us
  waiting for transfers between devices  232 us (67%)
  other arithmetic  34.2 us (10%)
  matrix products  26.9 us (8%)
  blocking collectives  19.7 us (6%)
  local copies, waits for them, and re-layouts  17.6 us (5%)
  starting transfers between devices  15.2 us (4%)
    ppermute x6, waiting for transfers between devices, convolve(): lax.ppermute(line, ('tm', 'tile'), [(d, (d - have) % ways) for d in range...  148 us
    ppermute x2, waiting for transfers between devices, from_behind(): lax.ppermute(value, axis, [(source, source + steps) for source in range(f...  77.2 us
    dot_general x18, matrix products, convolve(): jnp.einsum('trwk,kn->trwn', widened[frame_off:frame_off + frames, row_off...  26.9 us
    concatenate x1, other arithmetic, convolve(): shard_piece = jnp.roll(line, here * lap, axis=2)  11.1 us
    dynamic_slice x2, local copies, waits for them, and re-layouts, convolve(): shard_piece = jnp.roll(line, here * lap, axis=2)  10.6 us
    psum x2, blocking collectives, normalize(): spread = lax.psum(jnp.sum(centered * centered, axis=(1, 3)), 'tile')  9.85 us
    psum x2, blocking collectives, normalize(): totals = lax.psum(jnp.sum(grouped, axis=(1, 3)), 'tile')  9.85 us
  transfers between devices with their start and end apart: 12, of which 9 were waited for; matrix products, arithmetic and copies ran while one was open for 6% of the time, Pallas kernels for 0%

profile of v1, /device:TPU:24, one launch (start us, length us, event | category | flops | bytes accessed | tf_op | source)
XLA Modules:
  0.0 345.9 jit_solution(9620271870141404566)
XLA Ops:
  0.0 1.5 convert_reduce_fusion
  1.7 4.9 %psum.28 = f32[2,32]{1,0:T(2,128)S(1)} all-reduce(f32[2,32]{1,0:T(2,128)S(1)} %reduce_sum.51), channel_id=1, replica_groups=mesh['tm'=4,'tile'=2,'clip'=4] {'tile'}, use_global_device_ids=true, to_apply=%region_2.0 | all-reduce | flops 64 | bytes 512 | tf_op jit(solution)/shard_map/psum | solution.py:33
  6.8 1.5 fusion.29
  8.5 4.9 %psum.29 = f32[2,32]{1,0:T(2,128)S(1)} all-reduce(f32[2,32]{1,0:T(2,128)S(1)} %reduce_sum.54), channel_id=1, replica_groups=mesh['tm'=4,'tile'=2,'clip'=4] {'tile'}, use_global_device_ids=true, to_apply=%region_5.6 | all-reduce | flops 64 | bytes 512 | tf_op jit(solution)/shard_map/psum | solution.py:36
  13.6 1.9 fusion.36
  16.8 3.7 %collective-permute-start.3 = (bf16[27,256,32]{1,2,0:T(8,128)(2,1)S(1)}, bf16[27,256,32]{1,2,0:T(8,128)(2,1)S(1)}, u32[]{:S(2)}, u32[]{:S(2)}) collective-permute-start(bf16[27,256,32]{1,2,0:T(8,128)(2,1)S(1)} %copy-done.3), channel_id=1, source_target_pairs={{0,28},{4,0},{8,4},{12,8},{16,12},{20,16},{24,20},{28,24},{1,29},{... | collective-permute-start | bytes 1327112 | tf_op jit(solution)/shard_map/ppermute | solution.py:66
  20.9 10.1 %collective-permute-done.3 = bf16[27,256,32]{1,2,0:T(8,128)(2,1)S(1)} collective-permute-done((bf16[27,256,32]{1,2,0:T(8,128)(2,1)S(1)}, bf16[27,256,32]{1,2,0:T(8,128)(2,1)S(1)}, u32[]{:S(2)}, u32[]{:S(2)}) %collective-permute-start.3) | collective-permute-done | bytes 442400 | tf_op jit(solution)/shard_map/ppermute | solution.py:66
  32.1 1.5 collective-permute-start.4
  33.6 53.8 %collective-permute-done = bf16[2,8,128,256]{3,2,1,0:T(8,128)(2,1)S(1)} collective-permute-done((bf16[2,8,128,256]{3,2,1,0:T(8,128)(2,1)S(1)}, bf16[2,8,128,256]{3,2,1,0:T(8,128)(2,1)S(1)}, u32[]{:S(2)}, u32[]{:S(2)}) %collective-permute-start) | collective-permute-done | bytes 1048608 | tf_op jit(solution)/shard_map/ppermute | solution.py:13
  88.2 2.0 collective-permute-start.1
  93.7 5.1 %collective-permute-done.2 = bf16[4,1,128,256]{3,2,1,0:T(8,128)(2,1)} collective-permute-done((bf16[4,1,128,256]{3,2,1,0:T(8,128)(2,1)}, bf16[4,1,128,256]{3,2,1,0:T(8,128)(2,1)}, u32[]{:S(2)}, u32[]{:S(2)}) %collective-permute-start.2) | collective-permute-done | bytes 262176 | tf_op jit(solution)/shard_map/ppermute | solution.py:24
  98.8 2.1 fusion.22
  102.4 15.7 %collective-permute-done.10 = bf16[27,256,64]{1,2,0:T(8,128)(2,1)} collective-permute-done((bf16[27,256,64]{1,2,0:T(8,128)(2,1)}, bf16[27,256,64]{1,2,0:T(8,128)(2,1)}, u32[]{:S(2)}, u32[]{:S(2)}) %collective-permute-start.10) | collective-permute-done | bytes 884768 | tf_op jit(solution)/shard_map/ppermute | solution.py:66
  119.4 1.9 fusion.63
  121.3 4.8 %pad_maximum_fusion = bf16[4,10,128,768]{3,2,1,0:T(8,128)(2,1)} fusion(bf16[4,10,128,256]{3,2,1,0:T(8,128)(2,1)S(1)} %get-tuple-element.9, bf16[4,1,128,256]{3,2,1,0:T(8,128)(2,1)} %collective-permute-done.2, bf16[2,8,128,256]{3,2,1,0:T(8,128)(2,1)S(1)} %fusion.36, bf16[2,8,128,256]{3,2,1,0:T(8,128)(2,1)S(1)} %collective-permute-done, ...), kind=kLoop, calls=%fused_computation.2 | loop fusion | flops 47185920 | bytes 15728640 | tf_op jit(solution)/shard_map/concatenate | solution.py:46
  126.1 84.4 %collective-permute-done.5 = bf16[27,256,128]{1,2,0:T(8,128)(2,1)S(1)} collective-permute-done((bf16[27,256,128]{1,2,0:T(8,128)(2,1)S(1)}, bf16[27,256,128]{1,2,0:T(8,128)(2,1)S(1)}, u32[]{:S(2)}, u32[]{:S(2)}) %collective-permute-start.5) | collective-permute-done | bytes 1769504 | tf_op jit(solution)/shard_map/ppermute | solution.py:66
  210.5 37.9 %collective-permute-done.11 = bf16[27,256,128]{1,2,0:T(8,128)(2,1)S(1)} collective-permute-done((bf16[27,256,128]{1,2,0:T(8,128)(2,1)S(1)}, bf16[27,256,128]{1,2,0:T(8,128)(2,1)S(1)}, u32[]{:S(2)}, u32[]{:S(2)}) %collective-permute-start.11) | collective-permute-done | bytes 1769504 | tf_op jit(solution)/shard_map/ppermute | solution.py:66
  248.4 11.1 %fusion.4 = (bf16[27,256,256]{1,2,0:T(8,128)(2,1)}, bf16[27,256,256]{1,2,0:T(8,128)(2,1)}) fusion(s32[]{:T(128)S(6)} %select_n.13, bf16[27,256,32]{1,2,0:T(8,128)(2,1)S(1)} %copy-done.2, bf16[27,256,32]{1,2,0:T(8,128)(2,1)S(1)} %copy-done.5, bf16[27,256,64]{1,2,0:T(8,128)(2,1)} %collective-permute-done.10, ...), kind=kLoop, calls=%fused_computation.24 | loop fusion | flops 56623104 | bytes 14155780 | tf_op jit(solution)/shard_map/jit(_roll_dynamic)/concatenate | solution.py:71
  259.5 4.6 %copy.10 = bf16[27,256,256]{2,1,0:T(8,128)(2,1)S(1)} copy(bf16[27,256,256]{1,2,0:T(8,128)(2,1)} %get-tuple-element.17) | data formatting | bytes 7077888 | tf_op jit(solution)/shard_map/jit(_roll_dynamic)/dynamic_slice | solution.py:71
  264.2 3.1 fusion.54
  267.2 3.1 fusion.55
  270.3 2.9 fusion.56
  278.3 2.5 convert_reduce_fusion.1
  280.9 4.9 %psum.30 = f32[2,32]{1,0:T(2,128)S(1)} all-reduce(f32[2,32]{1,0:T(2,128)S(1)} %reduce_sum.72), channel_id=1, replica_groups=mesh['tm'=4,'tile'=2,'clip'=4] {'tile'}, use_global_device_ids=true, to_apply=%region_8.10 | all-reduce | flops 64 | bytes 512 | tf_op jit(solution)/shard_map/psum | solution.py:33
  286.0 1.5 fusion.37
  287.7 4.9 %psum.31 = f32[2,32]{1,0:T(2,128)S(1)} all-reduce(f32[2,32]{1,0:T(2,128)S(1)} %reduce_sum.75), channel_id=1, replica_groups=mesh['tm'=4,'tile'=2,'clip'=4] {'tile'}, use_global_device_ids=true, to_apply=%region_11.13 | all-reduce | flops 64 | bytes 512 | tf_op jit(solution)/shard_map/psum | solution.py:36
  292.8 1.9 fusion.44
  296.0 23.5 %collective-permute-done.6 = bf16[2,8,128,256]{3,2,1,0:T(8,128)(2,1)S(1)} collective-permute-done((bf16[2,8,128,256]{3,2,1,0:T(8,128)(2,1)S(1)}, bf16[2,8,128,256]{3,2,1,0:T(8,128)(2,1)S(1)}, u32[]{:S(2)}, u32[]{:S(2)}) %collective-permute-start.6) | collective-permute-done | bytes 1048608 | tf_op jit(solution)/shard_map/ppermute | solution.py:13
  319.6 2.2 collective-permute-start.7
  323.0 5.9 %copy.11 = bf16[27,256,256]{2,1,0:T(8,128)(2,1)} copy(bf16[27,256,256]{1,2,0:T(8,128)(2,1)} %get-tuple-element.16) | data formatting | bytes 7077888 | tf_op jit(solution)/shard_map/jit(_roll_dynamic)/dynamic_slice | solution.py:71
  331.3 1.9 fusion.62
  343.3 2.6 fusion.45
  (77 shorter events, 31.2 us)
Async XLA Ops:
  0.0 16.8 %copy-start.3 = (bf16[27,256,32]{1,2,0:T(8,128)(2,1)S(1)}, bf16[27,256,32]{1,2,0:T(8,128)(2,1)}, u32[]{:S(2)}) copy-start(bf16[27,256,32]{1,2,0:T(8,128)(2,1)} %param.11) | copy-start | bytes 1327108
  0.0 20.4 %copy-start.2 = (bf16[27,256,32]{1,2,0:T(8,128)(2,1)S(1)}, bf16[27,256,32]{1,2,0:T(8,128)(2,1)}, u32[]{:S(2)}) copy-start(bf16[27,256,32]{1,2,0:T(8,128)(2,1)} %param.14) | copy-start | bytes 1327108
  15.5 71.9 %collective-permute-start = (bf16[2,8,128,256]{3,2,1,0:T(8,128)(2,1)S(1)}, bf16[2,8,128,256]{3,2,1,0:T(8,128)(2,1)S(1)}, u32[]{:S(2)}, u32[]{:S(2)}) collective-permute-start(bf16[2,8,128,256]{3,2,1,0:T(8,128)(2,1)S(1)} %fusion.36), channel_id=1, source_target_pairs={{0,8},{8,16},{16,24},{1,9},{9,17},{17,25},{2,10},{10,18},{18,26},{... | collective-permute-start | bytes 3145736 | tf_op jit(solution)/shard_map/ppermute | solution.py:13
  16.8 14.3 %collective-permute-start.3 = (bf16[27,256,32]{1,2,0:T(8,128)(2,1)S(1)}, bf16[27,256,32]{1,2,0:T(8,128)(2,1)S(1)}, u32[]{:S(2)}, u32[]{:S(2)}) collective-permute-start(bf16[27,256,32]{1,2,0:T(8,128)(2,1)S(1)} %copy-done.3), channel_id=1, source_target_pairs={{0,28},{4,0},{8,4},{12,8},{16,12},{20,16},{24,20},{28,24},{1,29},{... | collective-permute-start | bytes 1327112 | tf_op jit(solution)/shard_map/ppermute | solution.py:66
  20.5 71.1 %collective-permute-start.9 = (bf16[27,256,32]{1,2,0:T(8,128)(2,1)S(1)}, bf16[27,256,32]{1,2,0:T(8,128)(2,1)S(1)}, u32[]{:S(2)}, u32[]{:S(2)}) collective-permute-start(bf16[27,256,32]{1,2,0:T(8,128)(2,1)S(1)} %copy-done.2), channel_id=1, source_target_pairs={{0,28},{4,0},{8,4},{12,8},{16,12},{20,16},{24,20},{28,24},{1,29},{... | collective-permute-start | bytes 1327112 | tf_op jit(solution)/shard_map/ppermute | solution.py:66
  32.1 68.9 %collective-permute-start.4 = (bf16[27,256,64]{1,2,0:T(8,128)(2,1)}, bf16[27,256,64]{1,2,0:T(8,128)(2,1)}, u32[]{:S(2)}, u32[]{:S(2)}) collective-permute-start(bf16[27,256,64]{1,2,0:T(8,128)(2,1)} %pad_maximum_fusion.4), channel_id=1, source_target_pairs={{0,24},{4,28},{8,0},{12,4},{16,8},{20,12},{24,16},{28,20},{1,25},{... | collective-permute-start | bytes 2654216 | tf_op jit(solution)/shard_map/ppermute | solution.py:66
  88.2 5.5 %collective-permute-start.1 = (bf16[4,1,128,256]{3,2,1,0:T(8,128)(2,1)}, bf16[4,1,128,256]{3,2,1,0:T(8,128)(2,1)}, u32[]{:S(2)}, u32[]{:S(2)}) collective-permute-start(bf16[4,1,128,256]{3,2,1,0:T(8,128)(2,1)} %get-tuple-element.12), channel_id=1, source_target_pairs={{0,4},{1,5},{2,6},{3,7},{8,12},{9,13},{10,14},{11,15},{16,20},{17,... | collective-permute-start | bytes 786440 | tf_op jit(solution)/shard_map/ppermute | solution.py:21
  90.2 8.6 %collective-permute-start.2 = (bf16[4,1,128,256]{3,2,1,0:T(8,128)(2,1)}, bf16[4,1,128,256]{3,2,1,0:T(8,128)(2,1)}, u32[]{:S(2)}, u32[]{:S(2)}) collective-permute-start(bf16[4,1,128,256]{3,2,1,0:T(8,128)(2,1)} %get-tuple-element.13), channel_id=1, source_target_pairs={{4,0},{5,1},{6,2},{7,3},{12,8},{13,9},{14,10},{15,11},{20,16},{21,... | collective-permute-start | bytes 786440 | tf_op jit(solution)/shard_map/ppermute | solution.py:24
  91.5 0.8 copy-start.4
  93.3 24.8 %collective-permute-start.10 = (bf16[27,256,64]{1,2,0:T(8,128)(2,1)}, bf16[27,256,64]{1,2,0:T(8,128)(2,1)}, u32[]{:S(2)}, u32[]{:S(2)}) collective-permute-start(bf16[27,256,64]{1,2,0:T(8,128)(2,1)} %pad_maximum_fusion.5), channel_id=1, source_target_pairs={{0,24},{4,28},{8,0},{12,4},{16,8},{20,12},{24,16},{28,20},{1,25},{... | collective-permute-start | bytes 2654216 | tf_op jit(solution)/shard_map/ppermute | solution.py:66
  93.3 24.8 %copy-start.5 = (bf16[27,256,32]{1,2,0:T(8,128)(2,1)S(1)}, bf16[27,256,32]{1,2,0:T(8,128)(2,1)}, u32[]{:S(2)}) copy-start(bf16[27,256,32]{1,2,0:T(8,128)(2,1)} %copy-done.4) | copy-start | bytes 1327108
  102.3 108.2 %collective-permute-start.5 = (bf16[27,256,128]{1,2,0:T(8,128)(2,1)S(1)}, bf16[27,256,128]{1,2,0:T(8,128)(2,1)S(1)}, u32[]{:S(2)}, u32[]{:S(2)}) collective-permute-start(bf16[27,256,128]{1,2,0:T(8,128)(2,1)S(1)} %pad_maximum_fusion.2), channel_id=1, source_target_pairs={{0,16},{4,20},{8,24},{12,28},{16,0},{20,4},{24,8},{28,12},{1,17},{... | collective-permute-start | bytes 5308424 | tf_op jit(solution)/shard_map/ppermute | solution.py:66
  119.4 129.1 %collective-permute-start.11 = (bf16[27,256,128]{1,2,0:T(8,128)(2,1)S(1)}, bf16[27,256,128]{1,2,0:T(8,128)(2,1)S(1)}, u32[]{:S(2)}, u32[]{:S(2)}) collective-permute-start(bf16[27,256,128]{1,2,0:T(8,128)(2,1)S(1)} %pad_maximum_fusion.3), channel_id=1, source_target_pairs={{0,16},{4,20},{8,24},{12,28},{16,0},{20,4},{24,8},{28,12},{1,17},{... | collective-permute-start | bytes 5308424 | tf_op jit(solution)/shard_map/ppermute | solution.py:66
  264.2 9.1 %slice-start = ((s8[7864320]{0:T(1024)(128)(4,1)}), s8[4194304]{0:T(1024)(128)(4,1)S(1)}, s32[]{:S(2)}) async-start(s8[7864320]{0:T(1024)(128)(4,1)} %bitcast.148), calls=%async_computation | async-start | bytes 8388608
  267.2 6.0 %slice-start.1 = ((s8[7864320]{0:T(1024)(128)(4,1)}), s8[3670016]{0:T(1024)(128)(4,1)S(1)}, s32[]{:S(2)}) async-start(s8[7864320]{0:T(1024)(128)(4,1)} %bitcast.148), calls=%async_computation.1 | async-start | bytes 7340032
  277.2 1.0 copy-start.6
  278.2 14.6 %copy-start.8 = (f32[256]{0:T(256)S(1)}, f32[256]{0:T(256)}, u32[]{:S(2)}) copy-start(f32[256]{0:T(256)} %param.13) | copy-start | bytes 3076
  294.7 24.8 %collective-permute-start.6 = (bf16[2,8,128,256]{3,2,1,0:T(8,128)(2,1)S(1)}, bf16[2,8,128,256]{3,2,1,0:T(8,128)(2,1)S(1)}, u32[]{:S(2)}, u32[]{:S(2)}) collective-permute-start(bf16[2,8,128,256]{3,2,1,0:T(8,128)(2,1)S(1)} %fusion.44), channel_id=1, source_target_pairs={{0,8},{8,16},{16,24},{1,9},{9,17},{17,25},{2,10},{10,18},{18,26},{... | collective-permute-start | bytes 3145736 | tf_op jit(solution)/shard_map/ppermute | solution.py:13
  319.6 9.4 %collective-permute-start.7 = (bf16[4,1,128,256]{3,2,1,0:T(8,128)(2,1)S(1)}, bf16[4,1,128,256]{3,2,1,0:T(8,128)(2,1)S(1)}, u32[]{:S(2)}, u32[]{:S(2)}) collective-permute-start(bf16[4,1,128,256]{3,2,1,0:T(8,128)(2,1)S(1)} %get-tuple-element.10), channel_id=1, source_target_pairs={{0,4},{1,5},{2,6},{3,7},{8,12},{9,13},{10,14},{11,15},{16,20},{17,... | collective-permute-start | bytes 786440 | tf_op jit(solution)/shard_map/ppermute | solution.py:21
  321.7 8.3 %collective-permute-start.8 = (bf16[4,1,128,256]{3,2,1,0:T(8,128)(2,1)S(1)}, bf16[4,1,128,256]{3,2,1,0:T(8,128)(2,1)S(1)}, u32[]{:S(2)}, u32[]{:S(2)}) collective-permute-start(bf16[4,1,128,256]{3,2,1,0:T(8,128)(2,1)S(1)} %get-tuple-element.11), channel_id=1, source_target_pairs={{4,0},{5,1},{6,2},{7,3},{12,8},{13,9},{14,10},{15,11},{20,16},{21,... | collective-permute-start | bytes 786440 | tf_op jit(solution)/shard_map/ppermute | solution.py:24
  333.1 2.0 copy-start.1
  342.1 1.2 copy-start
  342.1 1.2 copy-start.7
